TPU v7x, 512 devices: a whole 4x8x8 slice. The times are simulated.
512 devices in a mesh: chan: 16 (over x, y_hi, core), tm: 32 (over z, y_lo).
Axes of the slice: x: 4, y: 8 (y_hi: 2, y_lo: 4; y = y_hi * 4 + y_lo), z: 8, core: 2. Of those that a mesh axis runs over, the one named last changes fastest.
Arguments:
- records: bfloat16 [2048, 491520], P('chan', 'tm'), may hold values from -6 to 6
- fir_taps: bfloat16 [257], replicated, may hold values from -0.375 to 0.375
- partners: int32 [1, 16], replicated, may hold values from 0 to 15, as said below
Outputs:
- cross: float32 [1, 2048, 6144], P(None, 'chan', 'tm')
Inputs may be any that keep to these rules, and one draw needn't show every extreme that they name: `partners`: each row is a permutation of the 16 blocks.
All inputs are finite; a program needn't handle non-finite values.
Results may differ from a plain program's by a relative error of at most 0.0003.
Values may be sent and summed in bfloat16 or wider, within the bound.
A program may use at most 64 MiB of HBM per device.

v0:
```python
import math

import jax
import jax.numpy as jnp
from jax import lax
from jax.sharding import PartitionSpec as P

WIN = 2560
NBIN = 24


first_bin = 4


def passed_along(shard, axis, by):
    count = lax.axis_size(axis)
    pairs = [(i, i + by) for i in range(count) if 0 <= i + by < count]
    return lax.ppermute(shard, axis, pairs)


def toeplitz(fir_taps):
    width = fir_taps.shape[0] - 1
    padded = jnp.concatenate(
        [jnp.zeros((width,), fir_taps.dtype), fir_taps, jnp.zeros((width - 1,), fir_taps.dtype)]
    )
    rolled = jnp.concatenate([padded[width:], padded[:width]])
    flat = jnp.tile(rolled, width)[: width * (3 * width - 1)]
    skewed = flat.reshape(width, 3 * width - 1)[:, : 2 * width]
    return skewed.T


def fourier_basis(win_len, tap_half, bins):
    times = jnp.arange(win_len, dtype=jnp.int32)
    freqs = jnp.arange(bins, dtype=jnp.int32) + first_bin
    phase_int = freqs[None, :] * times[:, None] % win_len
    angle = 2.0 * math.pi / win_len * phase_int.astype(jnp.float32)
    edge = jnp.minimum(times, win_len - 1 - times)
    ramp = jnp.sin(math.pi * (edge.astype(jnp.float32) + 0.5) / (2.0 * tap_half))
    taper = jnp.where(edge < tap_half, ramp * ramp, jnp.float32(1.0))
    scale = taper[:, None] / math.sqrt(win_len)
    return jnp.concatenate([scale * jnp.cos(angle), -scale * jnp.sin(angle)], axis=1)


def whiten(spectra, bins):
    real_part = spectra[..., :bins]
    imag_part = spectra[..., bins:]
    amplitude = jnp.sqrt(real_part * real_part + imag_part * imag_part + 1.0)
    return spectra / jnp.concatenate([amplitude, amplitude], axis=-1)


def cross_terms(left_spec, right_spec, bins):
    hi = lax.Precision.HIGHEST
    left_real, left_imag = (left_spec[..., :bins], left_spec[..., bins:])
    right_real, right_imag = (right_spec[..., :bins], right_spec[..., bins:])
    real_real = jnp.einsum("iwf,jwf->ijf", left_real, right_real, precision=hi)
    imag_imag = jnp.einsum("iwf,jwf->ijf", left_imag, right_imag, precision=hi)
    imag_real = jnp.einsum("iwf,jwf->ijf", left_imag, right_real, precision=hi)
    real_imag = jnp.einsum("iwf,jwf->ijf", left_real, right_imag, precision=hi)
    joined = jnp.stack([real_real + imag_imag, imag_real - real_imag], axis=2)
    return joined.reshape(left_spec.shape[0], right_spec.shape[0] * 2 * bins)


def shards(records, fir_taps, partners):
    hi = lax.Precision.HIGHEST
    chan_rows, local_len = records.shape
    tap_half = (fir_taps.shape[0] - 1) // 2
    block_len = 2 * tap_half
    hop_len = WIN // 2
    bins = NBIN
    window_count = local_len // hop_len
    lower_part = passed_along(records[:, local_len - tap_half :], "tm", 1)
    upper_part = passed_along(records[:, : hop_len + tap_half], "tm", -1)
    extended = jnp.concatenate([lower_part, records, upper_part], axis=1)
    block_count = (local_len + hop_len) // block_len
    pieces = extended.reshape(chan_rows, block_count + 1, block_len)
    stacked_in = jnp.concatenate([pieces[:, :-1], pieces[:, 1:]], axis=2)
    toeplitz_mat = toeplitz(fir_taps)
    filtered = jnp.einsum(
        "cnu,uv->cnv", stacked_in, toeplitz_mat, preferred_element_type=jnp.float32
    )
    by_hop = filtered.reshape(chan_rows, window_count + 1, hop_len)
    basis = fourier_basis(WIN, tap_half, bins)
    spectra = jnp.einsum("cwt,tq->cwq", by_hop[:, :-1], basis[:hop_len], precision=hi)
    spectra = spectra + jnp.einsum("cwt,tq->cwq", by_hop[:, 1:], basis[hop_len:], precision=hi)
    own_spec = whiten(spectra, bins)
    chan_index = lax.axis_index("chan")
    partner_ids = lax.dynamic_index_in_dim(partners, chan_index, 1, keepdims=False)
    shard_rows = lax.all_gather(own_spec, "chan", axis=0, tiled=True)
    row_count = shard_rows.shape[0]
    offset_row = partner_ids[0] * chan_rows
    inside = (offset_row >= 0) & (offset_row <= row_count - chan_rows)
    clamped = jnp.clip(offset_row, 0, row_count - chan_rows)
    taken_rows = lax.dynamic_slice_in_dim(shard_rows, clamped, chan_rows, 0)
    updated = [jnp.where(inside, taken_rows, jnp.float32(0.0))]
    partner_spec = jnp.stack(updated)
    tm_total = lax.axis_size("tm")
    norm_scale = 1.0 / math.sqrt(window_count * tm_total)
    partial_value = jnp.stack([cross_terms(own_spec, partner_spec[0], bins)])
    summed = lax.psum_scatter(partial_value, "tm", scatter_dimension=2, tiled=True)
    return summed * norm_scale


def solution(mesh):
    placed = (P("chan", "tm"), P(), P())
    return jax.shard_map(
        shards, mesh=mesh, in_specs=placed, out_specs=P(None, "chan", "tm"), check_vma=False
    )
```

profile of v0, /device:TPU:4, one launch (start us, length us, event | category | flops | bytes accessed | tf_op | source)
XLA Modules:
  0.0 355.1 jit_solution(13263036189496573414)
XLA Ops:
  6.5 0.0 copy-start
  6.5 0.0 all-gather.2.cloned.1.call-start
  6.5 6.3 %copy.12 = bf16[128,15360]{0,1:T(8,128)(2,1)} copy(bf16[128,15360]{1,0:T(8,128)(2,1)} %param.3) | data formatting | bytes 7864320 | tf_op args[0]
  12.8 1.0 slice.65
  13.8 1.3 collective-permute-start.1
  15.1 0.8 slice.64
  15.9 4.5 %collective-permute-start = (bf16[128,128]{0,1:T(8,128)(2,1)S(1)}, bf16[128,128]{0,1:T(8,128)(2,1)S(1)}, u32[]{:S(2)}, u32[]{:S(2)}) collective-permute-start(bf16[128,128]{0,1:T(8,128)(2,1)S(1)} %slice.64), channel_id=1, source_target_pairs={{0,1},{1,2},{2,3},{3,4},{4,5},{5,6},{6,7},{7,8},{8,9},{9,10},{10,1... | collective-permute-start | bytes 98312 | tf_op jit(solution)/shard_map/ppermute | solution.py:18
  20.5 0.1 select_multiply_fusion
  20.5 1.1 sine_multiply_fusion
  21.6 0.0 copy-done
  21.6 0.1 pad_maximum_fusion.3
  21.8 0.3 tile.10
  22.1 0.8 reshape.46
  22.9 0.0 collective-permute-done
  22.9 2.9 collective-permute-done.1
  25.9 9.8 %pad_maximum_fusion = bf16[128,16896]{0,1:T(8,128)(2,1)S(1)} fusion(bf16[128,1408]{0,1:T(8,128)(2,1)S(1)} %collective-permute-done.1, bf16[128,15360]{0,1:T(8,128)(2,1)} %copy.12, bf16[128,128]{0,1:T(8,128)(2,1)S(1)} %collective-permute-done), kind=kLoop, calls=%fused_computation.4 | loop fusion | flops 12976128 | bytes 8650752 | tf_op jit(solution)/shard_map/concatenate | solution.py:73
  35.7 4.3 %fusion.34 = (bf16[128,65,256]{0,2,1:T(8,128)(2,1)}, bf16[128,65,256]{0,2,1:T(8,128)(2,1)}) fusion(bf16[128,66,256]{0,2,1:T(8,128)(2,1)S(1)} %bitcast.25), kind=kLoop, calls=%fused_computation.55 | loop fusion | bytes 17039360 | tf_op jit(solution)/shard_map/slice | solution.py:76
  40.0 6.5 %copy.30 = bf16[128,65,256]{2,0,1:T(8,128)(2,1)} copy(bf16[128,65,256]{0,2,1:T(8,128)(2,1)} %get-tuple-element.5) | data formatting | bytes 8519680
  46.5 6.4 %copy.31 = bf16[128,65,256]{2,0,1:T(8,128)(2,1)} copy(bf16[128,65,256]{0,2,1:T(8,128)(2,1)} %get-tuple-element.6) | data formatting | bytes 8519680
  52.9 5.2 %fusion = f32[128,65,256]{0,2,1:T(8,128)S(1)} fusion(bf16[128,65,256]{2,0,1:T(8,128)(2,1)} %copy.31, bf16[128,65,256]{2,0,1:T(8,128)(2,1)} %copy.30, bf16[256,767]{1,0:T(8,128)(2,1)S(1)} %reshape.46), kind=kOutput, calls=%fused_computation | convolution fusion | flops 2198077440 | bytes 17301504 | tf_op jit(solution)/shard_map/cnu,uv->cnv/dot_general | solution.py:78
  58.1 5.0 %fusion.8 = f32[128,12,48]{0,2,1:T(8,128)S(1)} fusion(f32[128,13,1280]{0,2,1:T(8,128)S(1)} %bitcast.26, f32[2560,24]{0,1:T(8,128)S(1)} %get-tuple-element.12, f32[2560,24]{0,1:T(8,128)S(1)} %get-tuple-element.11), kind=kOutput, calls=%fused_computation.19 | convolution fusion | flops 1132523520 | bytes 9306112 | tf_op jit(solution)/shard_map/cwt,tq->cwq/dot_general | solution.py:83
  63.2 0.0 copy-start.1
  63.2 5.1 %convolution_add_fusion = f32[128,12,48]{0,2,1:T(8,128)S(1)} fusion(f32[128,12,48]{0,2,1:T(8,128)S(1)} %fusion.8, f32[128,13,1280]{0,2,1:T(8,128)S(1)} %bitcast.27, f32[2560,24]{0,1:T(8,128)S(1)} %get-tuple-element.11, f32[2560,24]{0,1:T(8,128)S(1)} %get-tuple-element.12), kind=kOutput, calls=%fused_computation.8 | convolution fusion | flops 1132597248 | bytes 9601024 | tf_op jit(solution)/shard_map/cwt,tq->cwq/dot_general | solution.py:84
  68.3 0.1 fusion.28
  68.3 0.8 maximum_divide_fusion
  69.1 0.0 all-gather.2.cloned.1.call-update
  69.1 0.3 reduce-scatter.2.cloned.1.call-start
  69.4 0.0 copy-done.1
  69.4 0.6 fusion.37
  71.9 1.0 fusion.35
  73.0 86.2 %all-gather.2.cloned.1.call-done = f32[2048,12,48]{0,2,1:T(8,128)} async-done(((f32[128,12,48]{0,2,1:T(8,128)}), f32[2048,12,48]{0,2,1:T(8,128)}) %all-gather.2.cloned.1.call-update) | async-done | bytes 4718608 | tf_op jit(solution)/shard_map/all_gather | solution.py:88
  159.2 1.1 dynamic-slice_select_fusion
  160.3 2.6 fusion.22
  163.0 2.6 fusion.16
  165.6 2.6 add_bitcast_fusion
  168.2 2.6 subtract_bitcast_fusion
  170.8 0.3 pad_maximum_fusion.1
  171.2 3.5 copy.28
  174.7 0.0 reduce-scatter.2.cloned.1.call-update
  174.7 172.1 %reduce-scatter.2.cloned.1.call-done = f32[1,128,192]{1,2,0:T(8,128)} async-done(((f32[1,128,6144]{1,2,0:T(8,128)}), f32[1,128,192]{1,2,0:T(8,128)}) %reduce-scatter.2.cloned.1.call-update) | async-done | bytes 98320 | tf_op jit(solution)/shard_map/reduce_scatter | solution.py:99
  346.7 1.5 broadcast_multiply_fusion
  (5 shorter events, 0.1 us)
Async XLA Ops:
  6.5 15.1 %copy-start = (bf16[257]{0:T(512)(128)(2,1)S(1)}, bf16[257]{0:T(512)(128)(2,1)}, u32[]{:S(2)}) copy-start(bf16[257]{0:T(512)(128)(2,1)} %param.4) | copy-start | bytes 1546
  6.5 152.7 %all-gather.2.cloned.1.call-start = ((), (), s32[]{:S(2)}) async-start(), calls=%async_computation.1 | async-start | bytes 5013504 | tf_op jit(solution)/shard_map/all_gather | solution.py:88
  13.8 12.0 %collective-permute-start.1 = (bf16[128,1408]{0,1:T(8,128)(2,1)S(1)}, bf16[128,1408]{0,1:T(8,128)(2,1)S(1)}, u32[]{:S(2)}, u32[]{:S(2)}) collective-permute-start(bf16[128,1408]{0,1:T(8,128)(2,1)S(1)} %slice.65), channel_id=1, source_target_pairs={{1,0},{2,1},{3,2},{4,3},{5,4},{6,5},{7,6},{8,7},{9,8},{10,9},{11,1... | collective-permute-start | bytes 1081352 | tf_op jit(solution)/shard_map/ppermute | solution.py:18
  15.9 7.0 %collective-permute-start = (bf16[128,128]{0,1:T(8,128)(2,1)S(1)}, bf16[128,128]{0,1:T(8,128)(2,1)S(1)}, u32[]{:S(2)}, u32[]{:S(2)}) collective-permute-start(bf16[128,128]{0,1:T(8,128)(2,1)S(1)} %slice.64), channel_id=1, source_target_pairs={{0,1},{1,2},{2,3},{3,4},{4,5},{5,6},{6,7},{7,8},{8,9},{9,10},{10,1... | collective-permute-start | bytes 98312 | tf_op jit(solution)/shard_map/ppermute | solution.py:18
  63.2 6.2 %copy-start.1 = (s32[1,16]{1,0:T(1,128)S(1)}, s32[1,16]{1,0:T(1,128)}, u32[]{:S(2)}) copy-start(s32[1,16]{1,0:T(1,128)} %param.5) | copy-start | bytes 196
  69.1 277.6 %reduce-scatter.2.cloned.1.call-start = ((), (), s32[]{:S(2)}) async-start(), calls=%async_computation.2 | async-start | bytes 3244032 | tf_op jit(solution)/shard_map/reduce_scatter | solution.py:99
Sparse Core Ops, SparseCore 0:
  69.2 89.9 all-gather.1
  174.8 171.8 reduce-scatter.1
where the time goes:
time: 356 us; the launch traced here: 355 us
  waiting for transfers between devices  261 us (73%)
  local copies, waits for them, and re-layouts  30.9 us (9%)
  matrix products  25.8 us (7%)
  other arithmetic  15.5 us (4%)
  between operations  15.5 us (4%)
  starting transfers between devices  6.09 us (2%)
    reduce_scatter x1, waiting for transfers between devices, shards(): lax.psum_scatter(partial_value, 'tm', scatter_dimension=2, tiled=True)  172 us
    all_gather x1, waiting for transfers between devices, shards(): shard_rows = lax.all_gather(own_spec, 'chan', axis=0, tiled=True)  86.2 us
    unnamed x7, local copies, waits for them, and re-layouts  19.2 us
    concatenate x1, other arithmetic, shards(): extended = jnp.concatenate([lower_part, records, upper_part], axis=1)  9.84 us
  transfers between devices with their start and end apart: 4, of which 3 were waited for; matrix products, arithmetic and copies ran while one was open for 1% of the time, Pallas kernels for 0%

commit v1 on v0

v1 whole, which is shorter than its diff:
```python
import functools
import math

import jax
import jax.numpy as jnp
import ml_dtypes
import numpy as np
from jax import lax
from jax.experimental import pallas as pl
from jax.experimental.pallas import tpu as pltpu
from jax.sharding import PartitionSpec as P

WIN = 2560
HOP = WIN // 2
NBIN = 24
HALF = 128
FIRST_BIN = 4
NQ = 2 * NBIN
CH = 128
LWIN = 12
ROWS = NBIN * 2 * LWIN
SPEC = 608
NX, NYH, NC = 4, 2, 2
NZ, NYL = 8, 4
NTM = NZ * NYL
JS = CH // NZ
GROUP = 3 * 2 * LWIN
PIECE = GROUP + 2 * LWIN
KDIM = NZ * 2 * LWIN
MESH = pl.DeviceIdType.MESH
NT = (((1,), (1,)), ((), ()))


def basis_table():
    t = np.arange(WIN)
    edge = np.minimum(t, WIN - 1 - t)
    ramp = np.sin(math.pi * (edge + 0.5) / (2.0 * HALF))
    taper = np.where(edge < HALF, ramp * ramp, 1.0) / math.sqrt(WIN)
    phase = (np.arange(NBIN)[:, None] + FIRST_BIN) * t[None, :] % WIN
    angle = 2.0 * math.pi / WIN * phase
    table = np.concatenate([np.cos(angle), -np.sin(angle)], axis=0) * taper
    table = np.pad(table, ((0, 0), (2 * HALF, 2 * HALF))).astype(np.float32)
    high = table.astype(ml_dtypes.bfloat16)
    low = (table - high.astype(np.float32)).astype(ml_dtypes.bfloat16)
    return np.concatenate([high, low], axis=0)


def split(value):
    high = value.astype(jnp.bfloat16)
    return high, (value - high.astype(jnp.float32)).astype(jnp.bfloat16)


def to_f32(codes):
    return codes.astype(jnp.int32).astype(jnp.float32)


def to_i16(value):
    return value.astype(jnp.int32).astype(jnp.int16)


def kernel(
    partners, taps, basis_hbm, x_hbm, out_ref,
    xs, basis, d_op, e_first, e_last, acc, up_send, low_send, up_recv, low_recv,
    coded, chan_got, z_got, a_val, sis_send, sis_recv, piece_send, piece_got,
    e_op, part_sum, part_got, flat, turned,
    x_sem, basis_sem, send_sem, recv_sem,
):
    ci, ti = lax.axis_index("chan"), lax.axis_index("tm")
    x, yh, core = ci // 4, (ci // 2) % 2, ci % 2
    z, yl = ti // NYL, ti % NYL

    def chan_id(xx, yy, cc):
        return (xx * 2 + yy) * 2 + cc

    def at_x(step):
        return (chan_id((x + step + NX) % NX, yh, core), ti)

    def at_z(step):
        return (ci, ((z + step + NZ) % NZ) * NYL + yl)

    def at_yl(step):
        return (ci, z * NYL + (yl + step) % NYL)

    def at_tm(step):
        return (ci, (ti + step + NTM) % NTM)

    across = (chan_id(x, 1 - yh, core), ti)
    sister = (chan_id(x, yh, 1 - core), ti)

    fetch_basis = pltpu.make_async_copy(basis_hbm, basis, basis_sem)
    fetch_basis.start()
    pair_order = [0, 5, 1, 2, 3, 4]

    def fetch(p):
        cols = pl.ds(2 * HOP * p, 2 * HOP)
        return pltpu.make_async_copy(x_hbm.at[:, cols], xs.at[:, cols], x_sem.at[p])

    for p in pair_order:
        fetch(p).start()

    barrier = pltpu.get_barrier_semaphore()
    peers = [at_tm(1), at_tm(-1), across, sister, at_x(1), at_x(-1)]
    peers += [at_z(d) for d in range(1, NZ)] + [at_yl(e) for e in range(1, NYL)]
    for peer in peers:
        pl.semaphore_signal(barrier, inc=1, device_id=peer, device_id_type=MESH)

    counter = [0]

    def send(src, dst, device):
        slot = counter[0]
        counter[0] += 1
        copy = pltpu.make_async_remote_copy(
            src_ref=src, dst_ref=dst, send_sem=send_sem.at[slot], recv_sem=recv_sem.at[slot],
            device_id=device, device_id_type=MESH,
        )
        copy.start()
        return copy

    sent = []

    acc[...] = jnp.zeros_like(acc)
    toep = pltpu.roll(jnp.broadcast_to(taps[...], (512, 512)), 0, 1, stride=1, stride_axis=0)
    toep = toep[:, :256].astype(jnp.bfloat16)
    fetch_basis.wait()
    for i in range(11):
        both = jnp.dot(
            basis[:, 256 * i : 256 * i + 512], toep, preferred_element_type=jnp.float32
        )
        high, low = split(both[:NQ] + both[NQ:])
        for half in range(2):
            j = 2 * i + half
            h_part = high[:, 128 * half : 128 * half + 128]
            l_part = low[:, 128 * half : 128 * half + 128]
            if j == 0:
                e_last[:NQ, :] = h_part
                e_last[NQ:, :] = l_part
            elif j == 21:
                e_first[:NQ, :] = h_part
                e_first[NQ:, :] = l_part
            else:
                row = 0 if j <= 10 else 2 * NQ
                col = 128 * ((j - 1) % 10)
                d_op[row : row + NQ, col : col + 128] = h_part
                d_op[row + NQ : row + 2 * NQ, col : col + 128] = l_part

    def hop_pair(p):
        fetch(p).wait()
        base = pl.multiple_of(2 * HOP * p, 128)
        second = pl.multiple_of(2 * HOP * p + HOP, 128)
        tail_a = pl.multiple_of(2 * HOP * p + HOP - 128, 128)
        tail_b = pl.multiple_of(2 * HOP * p + 2 * HOP - 128, 128)

        def both_hops(first, other, width):
            return jnp.concatenate([xs[:, pl.ds(first, width)], xs[:, pl.ds(other, width)]], axis=0)

        def product(left, right):
            return lax.dot_general(left, right, NT, preferred_element_type=jnp.float32)

        main = product(d_op[...], both_hops(base, second, HOP))
        first = product(e_first[...], both_hops(base, second, 128))
        last = product(e_last[...], both_hops(tail_a, tail_b, 128))
        p0 = main[:NQ] + main[NQ : 2 * NQ]
        p1 = main[2 * NQ : 3 * NQ] + main[3 * NQ :]
        p2 = first[:NQ] + first[NQ:]
        p3 = last[:NQ] + last[NQ:]
        for hop in range(2):
            lanes = slice(128 * hop, 128 * hop + 128)
            at = 2 * p + hop
            acc[at] += p2[:, lanes]
            acc[at + 1] += p1[:, lanes]
            acc[at + 2] += p0[:, lanes]
            acc[at + 3] += p3[:, lanes]

    hop_pair(0)
    hop_pair(5)
    up_send[...] = acc[0:2]
    low_send[...] = acc[14]
    pl.semaphore_wait(barrier, len(peers))
    up = send(up_send, up_recv, at_tm(-1))
    low = send(low_send, low_recv, at_tm(1))
    sent += [up, low]
    pl.loop(1, 5)(hop_pair)

    limit = jnp.float32(32767.0)

    def whiten(w):
        spec = acc[w + 2]
        real, imag = spec[:NBIN], spec[NBIN:]
        amp = jnp.sqrt(real * real + imag * imag + 1.0)
        real, imag = real / amp, imag / amp
        top = jnp.max(jnp.maximum(jnp.abs(real), jnp.abs(imag)), axis=0, keepdims=True)
        power = jnp.ceil(jnp.log2(jnp.maximum(top, 1e-30)))
        gain = limit / jnp.exp2(power)
        for part, value in enumerate((real, imag)):
            code = jnp.clip(jnp.floor(value * gain + 0.5), -limit, limit)
            coded[pl.ds(part * LWIN + w, NBIN, stride=2 * LWIN), :] = code
        coded[ROWS + w : ROWS + w + 1, :] = power
        coded[ROWS + LWIN + w : ROWS + LWIN + w + 1, :] = power

    for w in range(1, 10):
        whiten(w)
    coded[ROWS + 2 * LWIN :, :] = jnp.zeros((SPEC - ROWS - 2 * LWIN, CH), jnp.float32)
    up.wait_recv()
    low.wait_recv()
    acc[2] += jnp.where(ti > 0, 1.0, 0.0) * low_recv[...]
    acc[12:14] += jnp.where(ti < NTM - 1, 1.0, 0.0) * up_recv[...]
    for w in (0, 10, 11):
        whiten(w)
    own = chan_got.at[0]
    for r in range(0, SPEC, 32):
        chan_got[0, r : r + 32] = to_i16(coded[r : r + 32])

    def unpack_a(d, source, index):
        scale = jnp.exp2(to_f32(source[index, ROWS : ROWS + 32])[: 2 * LWIN]) * (1.0 / 32767.0)
        for i in range(NBIN // 2):
            block = to_f32(source[index, 48 * i : 48 * i + 48])
            a_val[2 * i, 24 * d : 24 * d + 24] = block[:24] * scale
            a_val[2 * i + 1, 24 * d : 24 * d + 24] = block[24:] * scale

    cut = SPEC // 2
    top, bottom = pl.ds(0, cut), pl.ds(cut, cut)

    def chan_slot(dx, dy):
        return chan_got.at[2 * dx + dy]

    y_top = send(own.at[top], chan_slot(0, 1).at[top], across)
    y_bottom = send(own.at[bottom], chan_slot(0, 1).at[bottom], across)
    x_right = send(own, chan_slot(1, 0), at_x(1))
    x_left = send(own, chan_slot(3, 0), at_x(-1))
    right = send(own, z_got.at[1], at_z(1))
    left = send(own, z_got.at[7], at_z(-1))
    sent += [y_top, y_bottom, x_right, x_left, right, left]
    unpack_a(0, chan_got, 0)

    def ring_step(step, right, left):
        right.wait_recv()
        left.wait_recv()
        if step < 3:
            right = send(z_got.at[step], z_got.at[step + 1], at_z(1))
            left = send(z_got.at[8 - step], z_got.at[7 - step], at_z(-1))
        else:
            right = send(z_got.at[3, top], z_got.at[4, top], at_z(1))
            left = send(z_got.at[5, bottom], z_got.at[4, bottom], at_z(-1))
        sent.extend([right, left])
        unpack_a(step, z_got, step)
        unpack_a(8 - step, z_got, 8 - step)
        return right, left

    x_right.wait_recv()
    x_left.wait_recv()
    far_top = send(chan_slot(1, 0).at[top], chan_slot(2, 0).at[top], at_x(1))
    far_bottom = send(chan_slot(3, 0).at[bottom], chan_slot(2, 0).at[bottom], at_x(-1))
    sent += [far_top, far_bottom]
    right, left = ring_step(1, right, left)
    right, left = ring_step(2, right, left)

    y_top.wait_recv()
    right_top = send(chan_slot(0, 1).at[top], chan_slot(1, 1).at[top], at_x(1))
    left_top = send(chan_slot(0, 1).at[top], chan_slot(3, 1).at[top], at_x(-1))
    y_bottom.wait_recv()
    right_bottom = send(chan_slot(0, 1).at[bottom], chan_slot(1, 1).at[bottom], at_x(1))
    left_bottom = send(chan_slot(0, 1).at[bottom], chan_slot(3, 1).at[bottom], at_x(-1))
    sent += [right_top, left_top, right_bottom, left_bottom]
    right, left = ring_step(3, right, left)
    right_top.wait_recv()
    across_top = send(chan_slot(1, 1).at[top], chan_slot(2, 1).at[top], at_x(1))
    left_top.wait_recv()
    right_bottom.wait_recv()
    left_bottom.wait_recv()
    across_bottom = send(chan_slot(3, 1).at[bottom], chan_slot(2, 1).at[bottom], at_x(-1))
    sent += [across_top, across_bottom]
    far_top.wait_recv()
    far_bottom.wait_recv()
    across_top.wait_recv()
    across_bottom.wait_recv()

    mine_at = partners[0, ci]
    theirs_at = partners[0, chan_id(x, yh, 1 - core)]

    def slot_of(block):
        dx = (x - block // 4 + NX) % NX
        dy = (yh + (block // 2) % 2) % 2
        return 2 * dx + dy

    sis_send[...] = chan_got[slot_of(theirs_at)]
    swap = send(sis_send, sis_recv, sister)
    sent.append(swap)
    swap.wait_recv()
    keep = jnp.where(mine_at % 2 == core, 1.0, 0.0)
    other = 1.0 - keep
    mine_slot = slot_of(mine_at)

    shift = (CH - JS * z) % CH
    group_of = lax.broadcasted_iota(jnp.int32, (24, CH), 1) // JS

    def chosen(row):
        picked = to_f32(chan_got[mine_slot, row : row + 48]) * keep
        picked = picked + to_f32(sis_recv[row : row + 48]) * other
        return pltpu.roll(picked, shift, 1)

    for i in range(NBIN // 2):
        coded[48 * i : 48 * i + 48] = chosen(48 * i)
    powers = to_f32(chan_got[mine_slot, ROWS : ROWS + 32]) * keep
    powers = powers + to_f32(sis_recv[ROWS : ROWS + 32]) * other
    coded[ROWS : ROWS + 32] = pltpu.roll(powers, shift, 1)

    def pack(d, carry):
        for r in range(0, PIECE, 24):
            piece = jnp.zeros((24, CH), jnp.float32)
            for g in range(NZ):
                row = GROUP * g + r if r < GROUP else ROWS
                moved = pltpu.roll(coded[row : row + 24], (JS * (g - d) + CH) % CH, 1)
                piece = jnp.where(group_of == g, moved, piece)
            turned[d, r : r + 24] = piece
        piece_send[d] = to_i16(turned[d])
        return carry

    lax.fori_loop(0, NZ, pack, 0)
    pieces = [send(piece_send.at[d], piece_got.at[d], at_z(d)) for d in range(1, NZ)]
    sent += pieces

    right.wait_recv()
    left.wait_recv()
    unpack_a(4, z_got, 4)

    row_of = lax.broadcasted_iota(jnp.int32, (24, CH), 0)
    sign = jnp.where(row_of < LWIN, -1.0, 1.0)
    for copy in pieces:
        copy.wait_recv()
    for d in range(NZ):
        codes = to_f32((piece_send if d == 0 else piece_got)[d])
        scale = jnp.exp2(codes[GROUP:]) * (1.0 / 32767.0)
        for k in range(3):
            value = codes[24 * k : 24 * k + 24] * scale
            flat[2 * k, 24 * d : 24 * d + 24] = value
            flat[2 * k + 1, 24 * d : 24 * d + 24] = pltpu.roll(value, LWIN, 0) * sign
    for k in range(3):
        for part in range(2):
            high, low = split(flat[2 * k + part].T)
            e_op[k, part] = high
            e_op[k, 2 + part] = low

    row8 = lax.broadcasted_iota(jnp.int32, (8, CH), 0)

    def bins(g, carry):
        rows = pl.ds(pl.multiple_of(JS * g, JS), JS)
        for k in range(3):
            f = 3 * g + k
            high, low = split(a_val[f])
            left_op = jnp.concatenate([e_op[k, n, rows] for n in range(4)], axis=0)
            got = jnp.dot(
                left_op, jnp.concatenate([high, low], axis=1), preferred_element_type=jnp.float32
            )
            got = got[:, :CH] + got[:, CH:]
            got = got[: 2 * JS] + got[2 * JS :]
            for n in range(2):
                re, im = got[8 * n : 8 * n + 8], got[JS + 8 * n : JS + 8 * n + 8]
                part_sum[2 * n, f] = jnp.where(row8 < 4, re, pltpu.roll(im, 4, 0))
                part_sum[2 * n + 1, f] = jnp.where(row8 < 4, pltpu.roll(re, 4, 0), im)
        return carry

    lax.fori_loop(0, NZ, bins, 0)
    sums = [
        send(part_sum.at[(yl + e) % NYL], part_got.at[e - 1], at_yl(e)) for e in range(1, NYL)
    ]
    sent += sums
    for copy in sums:
        copy.wait_recv()
    norm = 1.0 / math.sqrt(LWIN * NTM)
    total = (part_sum[yl] + part_got[0]) + (part_got[1] + part_got[2])
    flat[0] = (total * norm).reshape(KDIM, CH)
    for j in range(4):
        for part in range(2):
            rows = flat[0, pl.ds(4 * part + j, NBIN, stride=8), :]
            at = 24 * (2 * j + part)
            flat[1, at : at + 24] = rows
    out_ref[0] = flat[1].T
    for copy in sent:
        copy.wait_send()


def shards(records, fir_taps, partners):
    taps = fir_taps.astype(jnp.float32)
    line = jnp.concatenate([taps[256:], jnp.zeros((255,), jnp.float32), taps[:256]])
    line = line.reshape(1, 512)
    f32, bf16, i16 = jnp.float32, jnp.bfloat16, jnp.int16
    vmem = pltpu.VMEM
    copies = 2 + 2 + 4 + 8 + 2 + 4 + 2 + 1 + 7 + 3 + 4
    return pl.pallas_call(
        kernel,
        out_shape=jax.ShapeDtypeStruct((1, CH, KDIM), f32),
        in_specs=[
            pl.BlockSpec(memory_space=pltpu.SMEM),
            pl.BlockSpec(memory_space=pltpu.VMEM),
            pl.BlockSpec(memory_space=pl.ANY),
            pl.BlockSpec(memory_space=pl.ANY),
        ],
        out_specs=pl.BlockSpec(memory_space=pltpu.VMEM),
        scratch_shapes=[
            vmem((CH, LWIN * HOP), bf16),
            vmem((2 * NQ, WIN + 4 * HALF), bf16),
            vmem((4 * NQ, HOP), bf16),
            vmem((2 * NQ, 128), bf16),
            vmem((2 * NQ, 128), bf16),
            vmem((16, NQ, CH), f32),
            vmem((2, NQ, CH), f32),
            vmem((NQ, CH), f32),
            vmem((2, NQ, CH), f32),
            vmem((NQ, CH), f32),
            vmem((SPEC, CH), f32),
            vmem((8, SPEC, CH), i16),
            vmem((NZ, SPEC, CH), i16),
            vmem((NBIN, KDIM, CH), f32),
            vmem((SPEC, CH), i16),
            vmem((SPEC, CH), i16),
            vmem((NZ, PIECE, CH), i16),
            vmem((NZ, PIECE, CH), i16),
            vmem((3, 4, CH, KDIM), bf16),
            vmem((NYL, NBIN, 8, CH), f32),
            vmem((NYL - 1, NBIN, 8, CH), f32),
            vmem((6, KDIM, CH), f32),
            vmem((NZ, PIECE, CH), f32),
            pltpu.SemaphoreType.DMA((6,)),
            pltpu.SemaphoreType.DMA,
            pltpu.SemaphoreType.DMA((copies,)),
            pltpu.SemaphoreType.DMA((copies,)),
        ],
        compiler_params=pltpu.CompilerParams(collective_id=0, has_side_effects=True),
    )(partners, line, jnp.asarray(basis_table()), records)


def solution(mesh):
    placed = (P("chan", "tm"), P(), P())
    return jax.shard_map(
        shards, mesh=mesh, in_specs=placed, out_specs=P(None, "chan", "tm"), check_vma=False
    )
```

time: 356 us -> 66.6 us (0.19)
  the two profiles are of different devices: /device:TPU:4 before, /device:TPU:57 now
where the time goes in v1:
time: 66.6 us; the launch traced here: 66.4 us
  Pallas kernels  61.4 us (92%)
  local copies, waits for them, and re-layouts  3.6 us (5%)
  other arithmetic  1.34 us (2%)
    pallas_call x1, Pallas kernels, shards(): pl.pallas_call(kernel, out_shape=jax.ShapeDtypeStruct((1, CH, KDIM), f32)...  61.4 us
    pallas_call x1, local copies, waits for them, and re-layouts, shards(): pl.pallas_call(kernel, out_shape=jax.ShapeDtypeStruct((1, CH, KDIM), f32)...  1.64 us
    concatenate x1, other arithmetic, shards(): jnp.concatenate([taps[256:], jnp.zeros((255,), jnp.float32), taps[:256]])  1.34 us

profile of v1, /device:TPU:57, one launch (start us, length us, event | category | flops | bytes accessed | tf_op | source)
XLA Modules:
  0.0 66.4 jit_solution(11636776869202821341)
XLA Ops:
  0.0 1.3 %slice.6 = f32[1]{0:T(128)} slice(bf16[257]{0:T(512)(128)(2,1)} %param.5), slice={[256:257]} | slice | bytes 8 | tf_op jit(solution)/shard_map/slice | solution.py:384
  1.3 0.7 %slice.7 = f32[256]{0:T(256)S(1)} slice(bf16[257]{0:T(512)(128)(2,1)} %param.5), slice={[0:256]} | slice | bytes 2048 | tf_op jit(solution)/shard_map/slice | solution.py:384
  2.0 1.3 %pad_maximum_fusion = f32[512]{0:T(512)} fusion(f32[256]{0:T(256)S(1)} %slice.7, f32[255]{0:T(256)S(1)} %broadcast_in_dim.3, f32[1]{0:T(128)} %slice.6), kind=kLoop, calls=%fused_computation | loop fusion | flops 1024 | bytes 4096 | tf_op jit(solution)/shard_map/concatenate | solution.py:384
  3.3 61.4 %shard_map.46 = f32[1,128,192]{2,1,0:T(8,128)} custom-call(s32[1,16]{1,0:T(1,128)} %partners.1, f32[1,512]{1,0:T(1,128)} %bitcast.1, bf16[96,3072]{1,0:T(8,128)(2,1)} %constant.4.clone.basis_hbm, bf16[128,15360]{1,0:T(8,128)(2,1)} %x_hbm.1), custom_call_target="tpu_custom_call" | custom-call | tf_op jit(solution)/shard_map/pallas_call | solution.py:389
  64.7 1.6 %copy.5 = f32[1,128,192]{1,2,0:T(8,128)} copy(f32[1,128,192]{2,1,0:T(8,128)} %shard_map.46) | data formatting | bytes 196608 | tf_op jit(solution)/shard_map/pallas_call | solution.py:389
  (1 shorter events, 0.0 us)

commit v2 on v1

--- a/solution.py
+++ b/solution.py
@@ -18,15 +18,18 @@
 NQ = 2 * NBIN
 CH = 128
 LWIN = 12
-ROWS = NBIN * 2 * LWIN
 SPEC = 608
 NX, NYH, NC = 4, 2, 2
 NZ, NYL = 8, 4
 NTM = NZ * NYL
 JS = CH // NZ
-GROUP = 3 * 2 * LWIN
-PIECE = GROUP + 2 * LWIN
+PIECE = 96
 KDIM = NZ * 2 * LWIN
+COUNTS = (8, 4)
+BASES = (0, 400)
+CHUNKS = (pl.ds(0, 400), pl.ds(400, 208))
+HEAD, TAIL = pl.ds(0, 304), pl.ds(304, 96)
+BLOCKS = ((0, 80), (80, 80), (160, 80), (240, 80), (320, 80), (400, 112), (512, 96))
 MESH = pl.DeviceIdType.MESH
 NT = (((1,), (1,)), ((), ()))
 
@@ -61,8 +64,8 @@
 def kernel(
     partners, taps, basis_hbm, x_hbm, out_ref,
     xs, basis, d_op, e_first, e_last, acc, up_send, low_send, up_recv, low_recv,
-    coded, chan_got, z_got, a_val, sis_send, sis_recv, piece_send, piece_got,
-    e_op, part_sum, part_got, flat, turned,
+    coded, chan_a, chan_b, z_got, a_val, sis_send, sis_recv, piece_send, piece_got,
+    e_op, part_sum, part_got, flat, turned, line,
     x_sem, basis_sem, send_sem, recv_sem,
 ):
     ci, ti = lax.axis_index("chan"), lax.axis_index("tm")
@@ -114,12 +117,17 @@
             device_id=device, device_id_type=MESH,
         )
         copy.start()
+        sent.append(copy)
         return copy
 
     sent = []
 
     acc[...] = jnp.zeros_like(acc)
-    toep = pltpu.roll(jnp.broadcast_to(taps[...], (512, 512)), 0, 1, stride=1, stride_axis=0)
+    row = taps[...].astype(jnp.float32).reshape(1, 257)
+    line[...] = jnp.zeros_like(line)
+    line[:, 256:] = row[:, :256]
+    line[:, :1] = row[:, 256:]
+    toep = pltpu.roll(jnp.broadcast_to(line[...], (512, 512)), 0, 1, stride=1, stride_axis=0)
     toep = toep[:, :256].astype(jnp.bfloat16)
     fetch_basis.wait()
     for i in range(11):
@@ -178,12 +186,12 @@
     pl.semaphore_wait(barrier, len(peers))
     up = send(up_send, up_recv, at_tm(-1))
     low = send(low_send, low_recv, at_tm(1))
-    sent += [up, low]
     pl.loop(1, 5)(hop_pair)
 
     limit = jnp.float32(32767.0)
 
-    def whiten(w):
+    def whiten(w, chunk, i):
+        base, n = BASES[chunk], COUNTS[chunk]
         spec = acc[w + 2]
         real, imag = spec[:NBIN], spec[NBIN:]
         amp = jnp.sqrt(real * real + imag * imag + 1.0)
@@ -193,86 +201,112 @@
         gain = limit / jnp.exp2(power)
         for part, value in enumerate((real, imag)):
             code = jnp.clip(jnp.floor(value * gain + 0.5), -limit, limit)
-            coded[pl.ds(part * LWIN + w, NBIN, stride=2 * LWIN), :] = code
-        coded[ROWS + w : ROWS + w + 1, :] = power
-        coded[ROWS + LWIN + w : ROWS + LWIN + w + 1, :] = power
-
-    for w in range(1, 10):
-        whiten(w)
-    coded[ROWS + 2 * LWIN :, :] = jnp.zeros((SPEC - ROWS - 2 * LWIN, CH), jnp.float32)
-    up.wait_recv()
+            coded[pl.ds(base + part * n + i, NBIN, stride=2 * n), :] = code
+            at = base + NQ * n + part * n + i
+            coded[at : at + 1, :] = power
+
+    chan_got = (chan_a, chan_b)
+
+    def chan_slot(dx, dy, chunk):
+        return chan_got[chunk].at[2 * dx + dy]
+
+    def launch(chunk):
+        rows = CHUNKS[chunk]
+        own = chan_slot(0, 0, chunk)
+        return [
+            send(own, chan_slot(0, 1, chunk), across),
+            send(own, z_got.at[1, rows], at_z(1)),
+            send(own, z_got.at[7, rows], at_z(-1)),
+            send(own, chan_slot(1, 0, chunk), at_x(1)),
+            send(own, chan_slot(3, 0, chunk), at_x(-1)),
+        ]
+
+    for i in range(8):
+        whiten(i + 1, 0, i)
+    for r, size in BLOCKS[:5]:
+        chan_a[0, r : r + size] = to_i16(coded[r : r + size])
+    first = launch(0)
+    coded[600:, :] = jnp.zeros((8, CH), jnp.float32)
+    whiten(9, 1, 1)
     low.wait_recv()
     acc[2] += jnp.where(ti > 0, 1.0, 0.0) * low_recv[...]
+    whiten(0, 1, 0)
+    up.wait_recv()
     acc[12:14] += jnp.where(ti < NTM - 1, 1.0, 0.0) * up_recv[...]
-    for w in (0, 10, 11):
-        whiten(w)
-    own = chan_got.at[0]
-    for r in range(0, SPEC, 32):
-        chan_got[0, r : r + 32] = to_i16(coded[r : r + 32])
-
-    def unpack_a(d, source, index):
-        scale = jnp.exp2(to_f32(source[index, ROWS : ROWS + 32])[: 2 * LWIN]) * (1.0 / 32767.0)
-        for i in range(NBIN // 2):
-            block = to_f32(source[index, 48 * i : 48 * i + 48])
-            a_val[2 * i, 24 * d : 24 * d + 24] = block[:24] * scale
-            a_val[2 * i + 1, 24 * d : 24 * d + 24] = block[24:] * scale
-
-    cut = SPEC // 2
-    top, bottom = pl.ds(0, cut), pl.ds(cut, cut)
-
-    def chan_slot(dx, dy):
-        return chan_got.at[2 * dx + dy]
-
-    y_top = send(own.at[top], chan_slot(0, 1).at[top], across)
-    y_bottom = send(own.at[bottom], chan_slot(0, 1).at[bottom], across)
-    x_right = send(own, chan_slot(1, 0), at_x(1))
-    x_left = send(own, chan_slot(3, 0), at_x(-1))
-    right = send(own, z_got.at[1], at_z(1))
-    left = send(own, z_got.at[7], at_z(-1))
-    sent += [y_top, y_bottom, x_right, x_left, right, left]
-    unpack_a(0, chan_got, 0)
-
-    def ring_step(step, right, left):
+    whiten(10, 1, 2)
+    whiten(11, 1, 3)
+    for r, size in BLOCKS[5:]:
+        chan_b[0, r - 400 : r - 400 + size] = to_i16(coded[r : r + size])
+    second = launch(1)
+    own_sent = (first, second)
+
+    def unpack_a(d, source, index, chunk, base=None):
+        base, n = BASES[chunk] if base is None else base, COUNTS[chunk]
+        at = 24 * d + 16 * chunk
+        power = to_f32(source[index, base + NQ * n : base + NQ * n + 16])
+        scale = jnp.exp2(power[: 2 * n]) * (1.0 / 32767.0)
+        for i in range(n // 2 * 6):
+            block = to_f32(source[index, base + 16 * i : base + 16 * i + 16])
+            for k in range(8 // n):
+                f = i * (8 // n) + k
+                a_val[f, at : at + 2 * n] = block[2 * n * k : 2 * n * k + 2 * n] * scale
+
+    def ring(step, chunk, right, left):
         right.wait_recv()
         left.wait_recv()
-        if step < 3:
-            right = send(z_got.at[step], z_got.at[step + 1], at_z(1))
-            left = send(z_got.at[8 - step], z_got.at[7 - step], at_z(-1))
-        else:
-            right = send(z_got.at[3, top], z_got.at[4, top], at_z(1))
-            left = send(z_got.at[5, bottom], z_got.at[4, bottom], at_z(-1))
-        sent.extend([right, left])
-        unpack_a(step, z_got, step)
-        unpack_a(8 - step, z_got, 8 - step)
+        rows = CHUNKS[chunk]
+        right = send(z_got.at[step, rows], z_got.at[step + 1, rows], at_z(1))
+        left = send(z_got.at[8 - step, rows], z_got.at[7 - step, rows], at_z(-1))
         return right, left
 
-    x_right.wait_recv()
-    x_left.wait_recv()
-    far_top = send(chan_slot(1, 0).at[top], chan_slot(2, 0).at[top], at_x(1))
-    far_bottom = send(chan_slot(3, 0).at[bottom], chan_slot(2, 0).at[bottom], at_x(-1))
-    sent += [far_top, far_bottom]
-    right, left = ring_step(1, right, left)
-    right, left = ring_step(2, right, left)
-
-    y_top.wait_recv()
-    right_top = send(chan_slot(0, 1).at[top], chan_slot(1, 1).at[top], at_x(1))
-    left_top = send(chan_slot(0, 1).at[top], chan_slot(3, 1).at[top], at_x(-1))
-    y_bottom.wait_recv()
-    right_bottom = send(chan_slot(0, 1).at[bottom], chan_slot(1, 1).at[bottom], at_x(1))
-    left_bottom = send(chan_slot(0, 1).at[bottom], chan_slot(3, 1).at[bottom], at_x(-1))
-    sent += [right_top, left_top, right_bottom, left_bottom]
-    right, left = ring_step(3, right, left)
-    right_top.wait_recv()
-    across_top = send(chan_slot(1, 1).at[top], chan_slot(2, 1).at[top], at_x(1))
-    left_top.wait_recv()
-    right_bottom.wait_recv()
-    left_bottom.wait_recv()
-    across_bottom = send(chan_slot(3, 1).at[bottom], chan_slot(2, 1).at[bottom], at_x(-1))
-    sent += [across_top, across_bottom]
-    far_top.wait_recv()
-    far_bottom.wait_recv()
-    across_top.wait_recv()
-    across_bottom.wait_recv()
+    def far_z(chunk):
+        if chunk == 0:
+            return [
+                send(z_got.at[3, HEAD], z_got.at[4, HEAD], at_z(1)),
+                send(z_got.at[5, TAIL], z_got.at[4, TAIL], at_z(-1)),
+            ]
+        rows = CHUNKS[1]
+        return [send(z_got.at[5, rows], z_got.at[4, rows], at_z(-1))]
+
+    def far_x(dy, chunk):
+        before, after, target = [chan_slot(dx, dy, chunk) for dx in (1, 3, 2)]
+        if chunk == 0:
+            return [
+                send(before.at[HEAD], target.at[HEAD], at_x(1)),
+                send(after.at[TAIL], target.at[TAIL], at_x(-1)),
+            ]
+        return [send(after, target, at_x(-1))]
+
+    zr, zl = [None, None], [None, None]
+    far_own = []
+    for c in range(2):
+        zr[c], zl[c] = ring(1, c, own_sent[c][1], own_sent[c][2])
+        own_sent[c][3].wait_recv()
+        own_sent[c][4].wait_recv()
+        far_own += far_x(0, c)
+        unpack_a(0, chan_got[c], 0, c, 0)
+    by_x = []
+    for c in range(2):
+        own_sent[c][0].wait_recv()
+        by_x.append((
+            send(chan_slot(0, 1, c), chan_slot(1, 1, c), at_x(1)),
+            send(chan_slot(0, 1, c), chan_slot(3, 1, c), at_x(-1)),
+        ))
+        unpack_a(1, z_got, 1, c)
+        unpack_a(7, z_got, 7, c)
+        zr[c], zl[c] = ring(2, c, zr[c], zl[c])
+    far_next = []
+    for c in range(2):
+        by_x[c][0].wait_recv()
+        by_x[c][1].wait_recv()
+        far_next.append(far_x(1, c))
+        unpack_a(2, z_got, 2, c)
+        unpack_a(6, z_got, 6, c)
+    zr[0].wait_recv()
+    zl[0].wait_recv()
+    last = far_z(0)
+    for copy in far_own:
+        copy.wait_recv()
 
     mine_at = partners[0, ci]
     theirs_at = partners[0, chan_id(x, yh, 1 - core)]
@@ -282,58 +316,85 @@
         dy = (yh + (block // 2) % 2) % 2
         return 2 * dx + dy
 
-    sis_send[...] = chan_got[slot_of(theirs_at)]
-    swap = send(sis_send, sis_recv, sister)
-    sent.append(swap)
-    swap.wait_recv()
+    theirs_slot = slot_of(theirs_at)
+    swaps = []
+    for c in range(2):
+        rows = CHUNKS[c]
+        for copy in far_next[c]:
+            copy.wait_recv()
+        for r, size in BLOCKS[:5] if c == 0 else BLOCKS[5:]:
+            at = r - BASES[c]
+            sis_send[r : r + size] = chan_got[c][theirs_slot, at : at + size]
+        swaps.append(send(sis_send.at[rows], sis_recv.at[rows], sister))
+        if c == 0:
+            zr[1].wait_recv()
+            zl[1].wait_recv()
+            last += far_z(1)
     keep = jnp.where(mine_at % 2 == core, 1.0, 0.0)
     other = 1.0 - keep
     mine_slot = slot_of(mine_at)
-
     shift = (CH - JS * z) % CH
-    group_of = lax.broadcasted_iota(jnp.int32, (24, CH), 1) // JS
-
-    def chosen(row):
-        picked = to_f32(chan_got[mine_slot, row : row + 48]) * keep
-        picked = picked + to_f32(sis_recv[row : row + 48]) * other
-        return pltpu.roll(picked, shift, 1)
-
-    for i in range(NBIN // 2):
-        coded[48 * i : 48 * i + 48] = chosen(48 * i)
-    powers = to_f32(chan_got[mine_slot, ROWS : ROWS + 32]) * keep
-    powers = powers + to_f32(sis_recv[ROWS : ROWS + 32]) * other
-    coded[ROWS : ROWS + 32] = pltpu.roll(powers, shift, 1)
-
-    def pack(d, carry):
-        for r in range(0, PIECE, 24):
-            piece = jnp.zeros((24, CH), jnp.float32)
+
+    def pack(d, chunk):
+        base, n = BASES[chunk], COUNTS[chunk]
+        for r in range(0, 8 * n, 2 * n):
+            piece = jnp.zeros((2 * n, CH), jnp.float32)
+            group_of = lax.broadcasted_iota(jnp.int32, (2 * n, CH), 1) // JS
             for g in range(NZ):
-                row = GROUP * g + r if r < GROUP else ROWS
-                moved = pltpu.roll(coded[row : row + 24], (JS * (g - d) + CH) % CH, 1)
+                row = base + (6 * n * g + r if r < 6 * n else NQ * n)
+                moved = coded[row : row + 2 * n]
+                if g != d:
+                    moved = pltpu.roll(moved, (JS * (g - d) + CH) % CH, 1)
                 piece = jnp.where(group_of == g, moved, piece)
-            turned[d, r : r + 24] = piece
-        piece_send[d] = to_i16(turned[d])
-        return carry
-
-    lax.fori_loop(0, NZ, pack, 0)
-    pieces = [send(piece_send.at[d], piece_got.at[d], at_z(d)) for d in range(1, NZ)]
-    sent += pieces
-
-    right.wait_recv()
-    left.wait_recv()
-    unpack_a(4, z_got, 4)
-
-    row_of = lax.broadcasted_iota(jnp.int32, (24, CH), 0)
-    sign = jnp.where(row_of < LWIN, -1.0, 1.0)
-    for copy in pieces:
+            at = 64 * chunk + r
+            turned[d, at : at + 2 * n] = piece
+        rows = pl.ds(64 * chunk, 8 * n)
+        piece_send[d, rows] = to_i16(turned[d, rows])
+
+    pieces = []
+    for c in range(2):
+        swaps[c].wait_recv()
+        for r, size in BLOCKS[:5] if c == 0 else BLOCKS[5:]:
+            at = r - BASES[c]
+            picked = to_f32(chan_got[c][mine_slot, at : at + size]) * keep
+            picked = picked + to_f32(sis_recv[r : r + size]) * other
+            coded[r : r + size] = pltpu.roll(picked, shift, 1)
+        rows = pl.ds(64 * c, 8 * COUNTS[c])
+        batch = []
+        for d in (4, 3, 5, 2, 6, 1, 7):
+            pack(d, c)
+            batch.append((d, send(piece_send.at[d, rows], piece_got.at[d, rows], at_z(d))))
+        pack(0, c)
+        pieces.append(batch)
+    for c in range(2):
+        unpack_a(3, z_got, 3, c)
+        unpack_a(5, z_got, 5, c)
+    for copy in last:
         copy.wait_recv()
-    for d in range(NZ):
-        codes = to_f32((piece_send if d == 0 else piece_got)[d])
-        scale = jnp.exp2(codes[GROUP:]) * (1.0 / 32767.0)
+    unpack_a(4, z_got, 4, 0)
+    unpack_a(4, z_got, 4, 1)
+
+    sign = jnp.where(lax.broadcasted_iota(jnp.int32, (8, CH), 0) < 4, -1.0, 1.0)
+
+    def unpack_e(d, source, chunk):
+        n = COUNTS[chunk]
+        codes = to_f32(source[d, pl.ds(64 * chunk, 8 * n)])
+        scale = jnp.exp2(codes[6 * n :]) * (1.0 / 32767.0)
+        at = 24 * d + 16 * chunk
         for k in range(3):
-            value = codes[24 * k : 24 * k + 24] * scale
-            flat[2 * k, 24 * d : 24 * d + 24] = value
-            flat[2 * k + 1, 24 * d : 24 * d + 24] = pltpu.roll(value, LWIN, 0) * sign
+            value = codes[2 * n * k : 2 * n * k + 2 * n] * scale
+            flat[2 * k, at : at + 2 * n] = value
+            if chunk == 0:
+                flat[2 * k + 1, at : at + 8] = -value[8:]
+                flat[2 * k + 1, at + 8 : at + 16] = value[:8]
+            else:
+                flat[2 * k + 1, at : at + 8] = pltpu.roll(value, 4, 0) * sign
+
+    for c in range(2):
+        unpack_e(0, piece_send, c)
+        for d, copy in pieces[c][::-1]:
+            copy.wait_recv()
+            unpack_e(d, piece_got, c)
     for k in range(3):
         for part in range(2):
             high, low = split(flat[2 * k + part].T)
@@ -359,11 +420,15 @@
                 part_sum[2 * n + 1, f] = jnp.where(row8 < 4, pltpu.roll(re, 4, 0), im)
         return carry
 
-    lax.fori_loop(0, NZ, bins, 0)
-    sums = [
-        send(part_sum.at[(yl + e) % NYL], part_got.at[e - 1], at_yl(e)) for e in range(1, NYL)
-    ]
-    sent += sums
+    sums = []
+    for h in range(2):
+        lax.fori_loop(4 * h, 4 * h + 4, bins, 0)
+        bin_rows = pl.ds(12 * h, 12)
+        for e in (2, 1, 3):
+            target = (yl + e) % NYL
+            sums.append(
+                send(part_sum.at[target, bin_rows], part_got.at[e - 1, bin_rows], at_yl(e))
+            )
     for copy in sums:
         copy.wait_recv()
     norm = 1.0 / math.sqrt(LWIN * NTM)
@@ -380,12 +445,9 @@
 
 
 def shards(records, fir_taps, partners):
-    taps = fir_taps.astype(jnp.float32)
-    line = jnp.concatenate([taps[256:], jnp.zeros((255,), jnp.float32), taps[:256]])
-    line = line.reshape(1, 512)
     f32, bf16, i16 = jnp.float32, jnp.bfloat16, jnp.int16
     vmem = pltpu.VMEM
-    copies = 2 + 2 + 4 + 8 + 2 + 4 + 2 + 1 + 7 + 3 + 4
+    copies = 55
     return pl.pallas_call(
         kernel,
         out_shape=jax.ShapeDtypeStruct((1, CH, KDIM), f32),
@@ -408,7 +470,8 @@
             vmem((2, NQ, CH), f32),
             vmem((NQ, CH), f32),
             vmem((SPEC, CH), f32),
-            vmem((8, SPEC, CH), i16),
+            vmem((8, 400, CH), i16),
+            vmem((8, 208, CH), i16),
             vmem((NZ, SPEC, CH), i16),
             vmem((NBIN, KDIM, CH), f32),
             vmem((SPEC, CH), i16),
@@ -420,13 +483,14 @@
             vmem((NYL - 1, NBIN, 8, CH), f32),
             vmem((6, KDIM, CH), f32),
             vmem((NZ, PIECE, CH), f32),
+            vmem((1, 512), f32),
             pltpu.SemaphoreType.DMA((6,)),
             pltpu.SemaphoreType.DMA,
             pltpu.SemaphoreType.DMA((copies,)),
             pltpu.SemaphoreType.DMA((copies,)),
         ],
         compiler_params=pltpu.CompilerParams(collective_id=0, has_side_effects=True),
-    )(partners, line, jnp.asarray(basis_table()), records)
+    )(partners, fir_taps, jnp.asarray(basis_table()), records)
 
 
 def solution(mesh):

time: 66.6 us -> 57.8 us (0.87)
  the two profiles are of different devices: /device:TPU:57 before, /device:TPU:1 now
where the time goes in v2:
time: 57.8 us; the launch traced here: 57.7 us
  Pallas kernels  56 us (97%)
  local copies, waits for them, and re-layouts  1.64 us (3%)
    pallas_call x1, Pallas kernels, shards(): pl.pallas_call(kernel, out_shape=jax.ShapeDtypeStruct((1, CH, KDIM), f32)...  56 us
    pallas_call x1, local copies, waits for them, and re-layouts, shards(): pl.pallas_call(kernel, out_shape=jax.ShapeDtypeStruct((1, CH, KDIM), f32)...  1.64 us

profile of v2, /device:TPU:1, one launch (start us, length us, event | category | flops | bytes accessed | tf_op | source)
XLA Modules:
  0.0 57.7 jit_solution(17594122510620094129)
XLA Ops:
  0.0 56.0 %shard_map.46 = f32[1,128,192]{2,1,0:T(8,128)} custom-call(s32[1,16]{1,0:T(1,128)} %partners.1, bf16[257]{0:T(512)(128)(2,1)} %taps.1, bf16[96,3072]{1,0:T(8,128)(2,1)} %constant.2.clone.basis_hbm, bf16[128,15360]{1,0:T(8,128)(2,1)} %x_hbm.1), custom_call_target="tpu_custom_call" | custom-call | tf_op jit(solution)/shard_map/pallas_call | solution.py:451
  56.0 1.6 %copy.5 = f32[1,128,192]{1,2,0:T(8,128)} copy(f32[1,128,192]{2,1,0:T(8,128)} %shard_map.46) | data formatting | bytes 196608 | tf_op jit(solution)/shard_map/pallas_call | solution.py:451

commit v3 on v2

--- a/solution.py
+++ b/solution.py
@@ -65,7 +65,7 @@
     partners, taps, basis_hbm, x_hbm, out_ref,
     xs, basis, d_op, e_first, e_last, acc, up_send, low_send, up_recv, low_recv,
     coded, chan_a, chan_b, z_got, a_val, sis_send, sis_recv, piece_send, piece_got,
-    e_op, part_sum, part_got, flat, turned, line,
+    e_op, part_val, part_code, part_got, flat, turned, line,
     x_sem, basis_sem, send_sem, recv_sem,
 ):
     ci, ti = lax.axis_index("chan"), lax.axis_index("tm")
@@ -401,6 +401,9 @@
             e_op[k, part] = high
             e_op[k, 2 + part] = low
 
+    for n in range(NYL):
+        for h in range(2):
+            part_val[n, h, 96:] = jnp.zeros((16, CH), jnp.float32)
     row8 = lax.broadcasted_iota(jnp.int32, (8, CH), 0)
 
     def bins(g, carry):
@@ -414,26 +417,44 @@
             )
             got = got[:, :CH] + got[:, CH:]
             got = got[: 2 * JS] + got[2 * JS :]
+            tiles = []
             for n in range(2):
                 re, im = got[8 * n : 8 * n + 8], got[JS + 8 * n : JS + 8 * n + 8]
-                part_sum[2 * n, f] = jnp.where(row8 < 4, re, pltpu.roll(im, 4, 0))
-                part_sum[2 * n + 1, f] = jnp.where(row8 < 4, pltpu.roll(re, 4, 0), im)
+                tiles.append(jnp.where(row8 < 4, re, pltpu.roll(im, 4, 0)))
+                tiles.append(jnp.where(row8 < 4, pltpu.roll(re, 4, 0), im))
+            tops = [jnp.max(jnp.abs(tile), axis=0, keepdims=True) for tile in tiles]
+            power = jnp.ceil(jnp.log2(jnp.maximum(jnp.concatenate(tops, axis=0), 1e-30)))
+            gain = limit / jnp.exp2(power)
+            h, at = g // 4, f % 12
+            for n in range(NYL):
+                code = jnp.clip(jnp.floor(tiles[n] * gain[n : n + 1] + 0.5), -limit, limit)
+                part_val[n, h, pl.ds(pl.multiple_of(8 * at, 8), 8)] = code
+                part_val[n, h, pl.ds(96 + at, 1)] = power[n : n + 1]
         return carry
 
     sums = []
     for h in range(2):
         lax.fori_loop(4 * h, 4 * h + 4, bins, 0)
-        bin_rows = pl.ds(12 * h, 12)
+        for n in range(NYL):
+            part_code[n, h] = to_i16(part_val[n, h])
         for e in (2, 1, 3):
-            target = (yl + e) % NYL
             sums.append(
-                send(part_sum.at[target, bin_rows], part_got.at[e - 1, bin_rows], at_yl(e))
+                send(part_code.at[(yl + e) % NYL, h], part_got.at[e - 1, h], at_yl(e))
             )
-    for copy in sums:
-        copy.wait_recv()
     norm = 1.0 / math.sqrt(LWIN * NTM)
-    total = (part_sum[yl] + part_got[0]) + (part_got[1] + part_got[2])
-    flat[0] = (total * norm).reshape(KDIM, CH)
+
+    def decode(codes):
+        values = to_f32(codes)
+        scale = jnp.exp2(values[96:108]) * (norm / 32767.0)
+        return values[:96].reshape(12, 8, CH) * scale[:, None, :]
+
+    for h in range(2):
+        total = decode(part_code[yl, h])
+        for copy in sums[3 * h : 3 * h + 3]:
+            copy.wait_recv()
+        for e in range(NYL - 1):
+            total = total + decode(part_got[e, h])
+        flat[0, 96 * h : 96 * h + 96] = total.reshape(96, CH)
     for j in range(4):
         for part in range(2):
             rows = flat[0, pl.ds(4 * part + j, NBIN, stride=8), :]
@@ -479,8 +500,9 @@
             vmem((NZ, PIECE, CH), i16),
             vmem((NZ, PIECE, CH), i16),
             vmem((3, 4, CH, KDIM), bf16),
-            vmem((NYL, NBIN, 8, CH), f32),
-            vmem((NYL - 1, NBIN, 8, CH), f32),
+            vmem((NYL, 2, 112, CH), f32),
+            vmem((NYL, 2, 112, CH), i16),
+            vmem((NYL - 1, 2, 112, CH), i16),
             vmem((6, KDIM, CH), f32),
             vmem((NZ, PIECE, CH), f32),
             vmem((1, 512), f32),

time: 57.8 us -> 55 us (0.952)
  Pallas kernels: 56 us -> 53.2 us
    pallas_call x1, Pallas kernels: 56 us -> 53.2 us  [shards(): pl.pallas_call(kernel, out_shape=jax.ShapeDtypeStruct((1, CH, KDIM), f32)...]
where the time goes in v3:
time: 55 us; the launch traced here: 54.8 us
  Pallas kernels  53.2 us (97%)
  local copies, waits for them, and re-layouts  1.64 us (3%)
    pallas_call x1, Pallas kernels, shards(): pl.pallas_call(kernel, out_shape=jax.ShapeDtypeStruct((1, CH, KDIM), f32)...  53.2 us
    pallas_call x1, local copies, waits for them, and re-layouts, shards(): pl.pallas_call(kernel, out_shape=jax.ShapeDtypeStruct((1, CH, KDIM), f32)...  1.64 us

profile of v3, /device:TPU:1, one launch (start us, length us, event | category | flops | bytes accessed | tf_op | source)
XLA Modules:
  0.0 54.8 jit_solution(5236318479015033977)
XLA Ops:
  0.0 53.2 %shard_map.46 = f32[1,128,192]{2,1,0:T(8,128)} custom-call(s32[1,16]{1,0:T(1,128)} %partners.1, bf16[257]{0:T(512)(128)(2,1)} %taps.1, bf16[96,3072]{1,0:T(8,128)(2,1)} %constant.2.clone.basis_hbm, bf16[128,15360]{1,0:T(8,128)(2,1)} %x_hbm.1), custom_call_target="tpu_custom_call" | custom-call | tf_op jit(solution)/shard_map/pallas_call | solution.py:472
  53.2 1.6 %copy.5 = f32[1,128,192]{1,2,0:T(8,128)} copy(f32[1,128,192]{2,1,0:T(8,128)} %shard_map.46) | data formatting | bytes 196608 | tf_op jit(solution)/shard_map/pallas_call | solution.py:472

commit v4 on v3

--- a/solution.py
+++ b/solution.py
@@ -102,7 +102,7 @@
         fetch(p).start()
 
     barrier = pltpu.get_barrier_semaphore()
-    peers = [at_tm(1), at_tm(-1), across, sister, at_x(1), at_x(-1)]
+    peers = [at_tm(1), at_tm(-1), across, sister, at_x(1), at_x(-1), at_x(2)]
     peers += [at_z(d) for d in range(1, NZ)] + [at_yl(e) for e in range(1, NYL)]
     for peer in peers:
         pl.semaphore_signal(barrier, inc=1, device_id=peer, device_id_type=MESH)
@@ -215,8 +215,11 @@
         own = chan_slot(0, 0, chunk)
         return [
             send(own, chan_slot(0, 1, chunk), across),
+            send(own, z_got.at[2, rows], at_z(2)),
+            send(own, z_got.at[6, rows], at_z(-2)),
             send(own, z_got.at[1, rows], at_z(1)),
             send(own, z_got.at[7, rows], at_z(-1)),
+            send(own, chan_slot(2, 0, chunk), at_x(2)),
             send(own, chan_slot(1, 0, chunk), at_x(1)),
             send(own, chan_slot(3, 0, chunk), at_x(-1)),
         ]
@@ -242,7 +245,7 @@
 
     def unpack_a(d, source, index, chunk, base=None):
         base, n = BASES[chunk] if base is None else base, COUNTS[chunk]
-        at = 24 * d + 16 * chunk
+        at = 16 * d if chunk == 0 else 128 + 8 * d
         power = to_f32(source[index, base + NQ * n : base + NQ * n + 16])
         scale = jnp.exp2(power[: 2 * n]) * (1.0 / 32767.0)
         for i in range(n // 2 * 6):
@@ -251,62 +254,36 @@
                 f = i * (8 // n) + k
                 a_val[f, at : at + 2 * n] = block[2 * n * k : 2 * n * k + 2 * n] * scale
 
-    def ring(step, chunk, right, left):
-        right.wait_recv()
-        left.wait_recv()
+    def pass_on(chunk):
         rows = CHUNKS[chunk]
-        right = send(z_got.at[step, rows], z_got.at[step + 1, rows], at_z(1))
-        left = send(z_got.at[8 - step, rows], z_got.at[7 - step, rows], at_z(-1))
-        return right, left
-
-    def far_z(chunk):
+        onward = [
+            send(z_got.at[2, rows], z_got.at[3, rows], at_z(1)),
+            send(z_got.at[6, rows], z_got.at[5, rows], at_z(-1)),
+        ]
         if chunk == 0:
-            return [
-                send(z_got.at[3, HEAD], z_got.at[4, HEAD], at_z(1)),
-                send(z_got.at[5, TAIL], z_got.at[4, TAIL], at_z(-1)),
-            ]
-        rows = CHUNKS[1]
-        return [send(z_got.at[5, rows], z_got.at[4, rows], at_z(-1))]
-
-    def far_x(dy, chunk):
-        before, after, target = [chan_slot(dx, dy, chunk) for dx in (1, 3, 2)]
-        if chunk == 0:
-            return [
-                send(before.at[HEAD], target.at[HEAD], at_x(1)),
-                send(after.at[TAIL], target.at[TAIL], at_x(-1)),
-            ]
-        return [send(after, target, at_x(-1))]
-
-    zr, zl = [None, None], [None, None]
-    far_own = []
-    for c in range(2):
-        zr[c], zl[c] = ring(1, c, own_sent[c][1], own_sent[c][2])
-        own_sent[c][3].wait_recv()
-        own_sent[c][4].wait_recv()
-        far_own += far_x(0, c)
+            onward.append(send(z_got.at[2, HEAD], z_got.at[4, HEAD], at_z(2)))
+            rows = TAIL
+        onward.append(send(z_got.at[6, rows], z_got.at[4, rows], at_z(-2)))
+        return onward
+
+    onward, by_x = [], []
+    for c in range(2):
+        own_sent[c][1].wait_recv()
+        own_sent[c][2].wait_recv()
+        onward.append(pass_on(c))
+        own_sent[c][0].wait_recv()
+        came = chan_slot(0, 1, c)
+        by_x.append([
+            send(came, chan_slot(2, 1, c), at_x(2)),
+            send(came, chan_slot(1, 1, c), at_x(1)),
+            send(came, chan_slot(3, 1, c), at_x(-1)),
+        ])
         unpack_a(0, chan_got[c], 0, c, 0)
-    by_x = []
-    for c in range(2):
-        own_sent[c][0].wait_recv()
-        by_x.append((
-            send(chan_slot(0, 1, c), chan_slot(1, 1, c), at_x(1)),
-            send(chan_slot(0, 1, c), chan_slot(3, 1, c), at_x(-1)),
-        ))
-        unpack_a(1, z_got, 1, c)
-        unpack_a(7, z_got, 7, c)
-        zr[c], zl[c] = ring(2, c, zr[c], zl[c])
-    far_next = []
-    for c in range(2):
-        by_x[c][0].wait_recv()
-        by_x[c][1].wait_recv()
-        far_next.append(far_x(1, c))
         unpack_a(2, z_got, 2, c)
         unpack_a(6, z_got, 6, c)
-    zr[0].wait_recv()
-    zl[0].wait_recv()
-    last = far_z(0)
-    for copy in far_own:
-        copy.wait_recv()
+    for c in range(2):
+        for copy in own_sent[c][3:]:
+            copy.wait_recv()
 
     mine_at = partners[0, ci]
     theirs_at = partners[0, chan_id(x, yh, 1 - core)]
@@ -320,16 +297,14 @@
     swaps = []
     for c in range(2):
         rows = CHUNKS[c]
-        for copy in far_next[c]:
+        for copy in by_x[c]:
             copy.wait_recv()
         for r, size in BLOCKS[:5] if c == 0 else BLOCKS[5:]:
             at = r - BASES[c]
             sis_send[r : r + size] = chan_got[c][theirs_slot, at : at + size]
         swaps.append(send(sis_send.at[rows], sis_recv.at[rows], sister))
-        if c == 0:
-            zr[1].wait_recv()
-            zl[1].wait_recv()
-            last += far_z(1)
+        unpack_a(1, z_got, 1, c)
+        unpack_a(7, z_got, 7, c)
     keep = jnp.where(mine_at % 2 == core, 1.0, 0.0)
     other = 1.0 - keep
     mine_slot = slot_of(mine_at)
@@ -367,12 +342,10 @@
         pack(0, c)
         pieces.append(batch)
     for c in range(2):
-        unpack_a(3, z_got, 3, c)
-        unpack_a(5, z_got, 5, c)
-    for copy in last:
-        copy.wait_recv()
-    unpack_a(4, z_got, 4, 0)
-    unpack_a(4, z_got, 4, 1)
+        for copy in onward[c]:
+            copy.wait_recv()
+        for d in (3, 5, 4):
+            unpack_a(d, z_got, d, c)
 
     sign = jnp.where(lax.broadcasted_iota(jnp.int32, (8, CH), 0) < 4, -1.0, 1.0)
 
@@ -380,7 +353,7 @@
         n = COUNTS[chunk]
         codes = to_f32(source[d, pl.ds(64 * chunk, 8 * n)])
         scale = jnp.exp2(codes[6 * n :]) * (1.0 / 32767.0)
-        at = 24 * d + 16 * chunk
+        at = 16 * d if chunk == 0 else 128 + 8 * d
         for k in range(3):
             value = codes[2 * n * k : 2 * n * k + 2 * n] * scale
             flat[2 * k, at : at + 2 * n] = value
@@ -395,11 +368,12 @@
         for d, copy in pieces[c][::-1]:
             copy.wait_recv()
             unpack_e(d, piece_got, c)
-    for k in range(3):
-        for part in range(2):
-            high, low = split(flat[2 * k + part].T)
-            e_op[k, part] = high
-            e_op[k, 2 + part] = low
+        depth = slice(0, 128) if c == 0 else slice(128, KDIM)
+        for k in range(3):
+            for part in range(2):
+                high, low = split(flat[2 * k + part, depth].T)
+                e_op[k, part, :, depth] = high
+                e_op[k, 2 + part, :, depth] = low
 
     for n in range(NYL):
         for h in range(2):

time: 55 us -> 53.6 us (0.975)
  Pallas kernels: 53.2 us -> 51.8 us
    pallas_call x1, Pallas kernels: 53.2 us -> 51.8 us  [shards(): pl.pallas_call(kernel, out_shape=jax.ShapeDtypeStruct((1, CH, KDIM), f32)...]
where the time goes in v4:
time: 53.6 us; the launch traced here: 53.4 us
  Pallas kernels  51.8 us (97%)
  local copies, waits for them, and re-layouts  1.64 us (3%)
    pallas_call x1, Pallas kernels, shards(): pl.pallas_call(kernel, out_shape=jax.ShapeDtypeStruct((1, CH, KDIM), f32)...  51.8 us
    pallas_call x1, local copies, waits for them, and re-layouts, shards(): pl.pallas_call(kernel, out_shape=jax.ShapeDtypeStruct((1, CH, KDIM), f32)...  1.64 us

profile of v4, /device:TPU:1, one launch (start us, length us, event | category | flops | bytes accessed | tf_op | source)
XLA Modules:
  0.0 53.4 jit_solution(15230906289837623984)
XLA Ops:
  0.0 51.8 %shard_map.46 = f32[1,128,192]{2,1,0:T(8,128)} custom-call(s32[1,16]{1,0:T(1,128)} %partners.1, bf16[257]{0:T(512)(128)(2,1)} %taps.1, bf16[96,3072]{1,0:T(8,128)(2,1)} %constant.2.clone.basis_hbm, bf16[128,15360]{1,0:T(8,128)(2,1)} %x_hbm.1), custom_call_target="tpu_custom_call" | custom-call | tf_op jit(solution)/shard_map/pallas_call | solution.py:446
  51.8 1.6 %copy.5 = f32[1,128,192]{1,2,0:T(8,128)} copy(f32[1,128,192]{2,1,0:T(8,128)} %shard_map.46) | data formatting | bytes 196608 | tf_op jit(solution)/shard_map/pallas_call | solution.py:446

commit v5 on v4

--- a/solution.py
+++ b/solution.py
@@ -28,6 +28,7 @@
 COUNTS = (8, 4)
 BASES = (0, 400)
 CHUNKS = (pl.ds(0, 400), pl.ds(400, 208))
+DEPTHS = (slice(0, 128), slice(128, 192))
 HEAD, TAIL = pl.ds(0, 304), pl.ds(304, 96)
 BLOCKS = ((0, 80), (80, 80), (160, 80), (240, 80), (320, 80), (400, 112), (512, 96))
 MESH = pl.DeviceIdType.MESH
@@ -65,7 +66,7 @@
     partners, taps, basis_hbm, x_hbm, out_ref,
     xs, basis, d_op, e_first, e_last, acc, up_send, low_send, up_recv, low_recv,
     coded, chan_a, chan_b, z_got, a_val, sis_send, sis_recv, piece_send, piece_got,
-    e_op, part_val, part_code, part_got, flat, turned, line,
+    e_op, part_val, part_code, part_got, flat, turned, line, a_op, early,
     x_sem, basis_sem, send_sem, recv_sem,
 ):
     ci, ti = lax.axis_index("chan"), lax.axis_index("tm")
@@ -346,6 +347,27 @@
             copy.wait_recv()
         for d in (3, 5, 4):
             unpack_a(d, z_got, d, c)
+        depth = DEPTHS[c]
+
+        def halve(f, carry):
+            high, low = split(a_val[f, depth])
+            a_op[f, depth, :CH] = high
+            a_op[f, depth, CH:] = low
+            return carry
+
+        lax.fori_loop(0, NBIN, halve, 0)
+
+    def product(g, k, depth):
+        rows = pl.ds(pl.multiple_of(JS * g, JS), JS)
+        left_op = jnp.concatenate([e_op[k, n, rows, depth] for n in range(4)], axis=0)
+        got = jnp.dot(left_op, a_op[3 * g + k, depth], preferred_element_type=jnp.float32)
+        got = got[:, :CH] + got[:, CH:]
+        return got[: 2 * JS] + got[2 * JS :]
+
+    def first_bins(g, carry):
+        for k in range(3):
+            early[3 * g + k] = product(g, k, DEPTHS[0])
+        return carry
 
     sign = jnp.where(lax.broadcasted_iota(jnp.int32, (8, CH), 0) < 4, -1.0, 1.0)
 
@@ -368,12 +390,14 @@
         for d, copy in pieces[c][::-1]:
             copy.wait_recv()
             unpack_e(d, piece_got, c)
-        depth = slice(0, 128) if c == 0 else slice(128, KDIM)
+        depth = DEPTHS[c]
         for k in range(3):
             for part in range(2):
                 high, low = split(flat[2 * k + part, depth].T)
                 e_op[k, part, :, depth] = high
                 e_op[k, 2 + part, :, depth] = low
+        if c == 0:
+            lax.fori_loop(0, NZ, first_bins, 0)
 
     for n in range(NYL):
         for h in range(2):
@@ -381,16 +405,9 @@
     row8 = lax.broadcasted_iota(jnp.int32, (8, CH), 0)
 
     def bins(g, carry):
-        rows = pl.ds(pl.multiple_of(JS * g, JS), JS)
         for k in range(3):
             f = 3 * g + k
-            high, low = split(a_val[f])
-            left_op = jnp.concatenate([e_op[k, n, rows] for n in range(4)], axis=0)
-            got = jnp.dot(
-                left_op, jnp.concatenate([high, low], axis=1), preferred_element_type=jnp.float32
-            )
-            got = got[:, :CH] + got[:, CH:]
-            got = got[: 2 * JS] + got[2 * JS :]
+            got = early[f] + product(g, k, DEPTHS[1])
             tiles = []
             for n in range(2):
                 re, im = got[8 * n : 8 * n + 8], got[JS + 8 * n : JS + 8 * n + 8]
@@ -480,6 +497,8 @@
             vmem((6, KDIM, CH), f32),
             vmem((NZ, PIECE, CH), f32),
             vmem((1, 512), f32),
+            vmem((NBIN, KDIM, 2 * CH), bf16),
+            vmem((NBIN, 2 * JS, CH), f32),
             pltpu.SemaphoreType.DMA((6,)),
             pltpu.SemaphoreType.DMA,
             pltpu.SemaphoreType.DMA((copies,)),

time: 53.6 us -> 53.1 us (level)
  no operation moved by 1% of the time
where the time goes in v5:
time: 53.1 us; the launch traced here: 53 us
  Pallas kernels  51.3 us (97%)
  local copies, waits for them, and re-layouts  1.64 us (3%)
    pallas_call x1, Pallas kernels, shards(): pl.pallas_call(kernel, out_shape=jax.ShapeDtypeStruct((1, CH, KDIM), f32)...  51.3 us
    pallas_call x1, local copies, waits for them, and re-layouts, shards(): pl.pallas_call(kernel, out_shape=jax.ShapeDtypeStruct((1, CH, KDIM), f32)...  1.64 us

profile of v5, /device:TPU:1, one launch (start us, length us, event | category | flops | bytes accessed | tf_op | source)
XLA Modules:
  0.0 53.0 jit_solution(3265933788196554753)
XLA Ops:
  0.0 51.3 %shard_map.46 = f32[1,128,192]{2,1,0:T(8,128)} custom-call(s32[1,16]{1,0:T(1,128)} %partners.1, bf16[257]{0:T(512)(128)(2,1)} %taps.1, bf16[96,3072]{1,0:T(8,128)(2,1)} %constant.2.clone.basis_hbm, bf16[128,15360]{1,0:T(8,128)(2,1)} %x_hbm.1), custom_call_target="tpu_custom_call" | custom-call | tf_op jit(solution)/shard_map/pallas_call | solution.py:463
  51.3 1.6 %copy.5 = f32[1,128,192]{1,2,0:T(8,128)} copy(f32[1,128,192]{2,1,0:T(8,128)} %shard_map.46) | data formatting | bytes 196608 | tf_op jit(solution)/shard_map/pallas_call | solution.py:463
